TPU v7x, 256 devices: a whole 4x4x8 slice. The times are simulated.
256 devices in a mesh: rhs: 32 (over x, z_lo, y), node: 8 (over z_hi, core).
Axes of the slice: x: 4, y: 4, z: 8 (z_hi: 4, z_lo: 2; z = z_hi * 2 + z_lo), core: 2. Of those that a mesh axis runs over, the one named last changes fastest.
Arguments:
- right_side: float32 [8192, 8192], P('node', 'rhs'), may hold values from -6 to 6
- diag_inv: float32 [32, 256, 256], P('node', 'rhs'), may hold values from -1 to 1
- lower: float32 [32, 256, 256], P('node', 'rhs'), may hold values from -0.4375 to 0.4375
- factor_pattern: int32 [32, 4, 4], P('node'), may hold values 0 or 1
- jacobian: float32 [32, 256, 768], P('node', 'rhs'), may hold values from -0.078125 to 0.078125
- jacobian_pattern: int32 [32, 4, 12], P('node'), may hold values 0 or 1
Outputs:
- solution: float32 [8192, 8192], P('node', 'rhs')
- residual: float32 [8192, 8192], P('node', 'rhs')
All inputs are finite; a program needn't handle non-finite values. No bound on the sum of `factor_pattern` or of `jacobian_pattern` on one device may be relied on, other than what follows from the above.
Results may differ from a plain program's by a relative error of at most 0.00021.
Values sent between devices are 32-bit elements; how exact they have to be, the bound alone decides.
A program may use at most 64 MiB of HBM per device.

v0:
```python
import jax
import jax.numpy as jnp
from jax import lax
from jax.sharding import PartitionSpec as P

HIGHEST_PREC = lax.Precision.HIGHEST
TRANSPOSED = (((0,), (0,)), ((), ()))


def shifted(value, axis, steps):
    count = lax.axis_size(axis)
    initial, last = (max(0, -steps), min(count, count - steps))
    return lax.ppermute(value, axis, [(source, source + steps) for source in range(initial, last)])


def extended(cells, sides, width):
    for axis, dim in sides:
        count = lax.axis_size(axis)
        ends = count - 1
        head = lax.slice_in_dim(cells, 0, width, axis=dim)
        tail = lax.slice_in_dim(cells, cells.shape[dim] - width, cells.shape[dim], axis=dim)
        cells = jnp.concatenate(
            [
                lax.ppermute(tail, axis, [(i, (i + 1) % count) for i in range(ends)]),
                cells,
                lax.ppermute(head, axis, [((i + 1) % count, i) for i in range(ends)]),
            ],
            axis=dim,
        )
    return cells


def apply_pattern(blocks, pattern):
    supers, row_count, col_count = blocks.shape
    block_size = row_count // pattern.shape[1]
    shaped = blocks.reshape(supers, pattern.shape[1], block_size, pattern.shape[2], block_size)
    weights = pattern.astype(jnp.float32)[:, :, None, :, None]
    return (shaped * weights).reshape(supers, row_count, col_count)


def sweep_down(inverse, masked, rhs_blocks, incoming):

    def advance(previous, inputs):
        inv_block, low_block, rhs_block = inputs
        coupled = jnp.dot(low_block, previous, precision=HIGHEST_PREC)
        solved = jnp.dot(inv_block, rhs_block - coupled, precision=HIGHEST_PREC)
        return (solved, solved)

    outgoing, values = lax.scan(advance, incoming, (inverse, masked, rhs_blocks))
    return (values, outgoing)


def sweep_up(inverse, masked, forward_blocks, incoming):

    def advance(entering, inputs):
        inv_block, low_block, forward_block = inputs
        solved = lax.dot_general(
            inv_block, forward_block - entering, TRANSPOSED, precision=HIGHEST_PREC
        )
        passed = lax.dot_general(low_block, solved, TRANSPOSED, precision=HIGHEST_PREC)
        return (passed, solved)

    outgoing, values = lax.scan(advance, incoming, (inverse, masked, forward_blocks), reverse=True)
    return (values, outgoing)


def jacobian_product(portion, pattern, windows):
    supers, row_count, col_count = portion.shape
    block_count = pattern.shape[1]
    block_size = col_count // pattern.shape[2]
    row_ids = lax.iota(jnp.int32, row_count)
    onehot = (row_ids[:, None] // block_size == lax.iota(jnp.int32, block_count)[None, :]).astype(
        jnp.float32
    )
    weights = jnp.einsum("ra,sac->src", onehot, pattern.astype(jnp.float32))
    shaped = portion.reshape(supers, row_count, pattern.shape[2], block_size)
    masked = (shaped * weights[:, :, :, None]).reshape(supers, row_count, col_count)
    return jnp.einsum("sij,sjr->sir", masked, windows, precision=HIGHEST_PREC)


def on_device(right_side, diag_inv, lower, factor_pattern, jacobian, jacobian_pattern):
    supers = diag_inv.shape[0]
    panel_rows = diag_inv.shape[2]
    columns = right_side.shape[1]
    rhs_blocks = right_side.reshape(supers, panel_rows, columns)
    inverse, lower_all = (
        lax.all_gather(diag_inv, "rhs", axis=1, tiled=True),
        lax.all_gather(lower, "rhs", axis=1, tiled=True),
    )
    masked = apply_pattern(lower_all, factor_pattern)
    zero_state = jnp.zeros((panel_rows, columns), jnp.float32)
    rounds = lax.axis_size("node")

    def relay_down(round_index, incoming):
        unused, outgoing = sweep_down(inverse, masked, rhs_blocks, incoming)
        return shifted(outgoing, "node", 1)

    incoming = lax.fori_loop(0, rounds - 1, relay_down, zero_state)
    forward, unused = sweep_down(inverse, masked, rhs_blocks, incoming)

    def relay_up(round_index, incoming):
        unused, outgoing = sweep_up(inverse, masked, forward, incoming)
        return shifted(outgoing, "node", -1)

    incoming = lax.fori_loop(0, rounds - 1, relay_up, zero_state)
    solution, unused = sweep_up(inverse, masked, forward, incoming)
    span = supers * panel_rows
    flattened = solution.reshape(span, columns)
    padded = extended(flattened, (("node", 0),), panel_rows)
    before = padded[:span].reshape(supers, panel_rows, columns)
    after = padded[2 * panel_rows :].reshape(supers, panel_rows, columns)
    windows = jnp.concatenate([before, solution, after], axis=1)
    product = jacobian_product(
        lax.all_gather(jacobian, "rhs", axis=1, tiled=True), jacobian_pattern, windows
    )
    residual = rhs_blocks - product
    return (flattened, residual.reshape(span, columns))


def solution(mesh):
    in_specs = (
        P("node", "rhs"),
        P("node", "rhs", None),
        P("node", "rhs", None),
        P("node", None, None),
        P("node", "rhs", None),
        P("node", None, None),
    )
    out_specs = (P("node", "rhs"), P("node", "rhs"))
    return jax.shard_map(
        on_device, mesh=mesh, in_specs=in_specs, out_specs=out_specs, check_vma=False
    )
```

profile of v0, /device:TPU:1, one launch (start us, length us, event | category | flops | bytes accessed | tf_op | source)
XLA Modules:
  0.0 639.9 jit_solution(5976639583881987861)
XLA Ops:
  13.5 131.2 %all-gather.4.cloned.1.call-done = f32[4,256,256]{2,1,0:T(8,128)} async-done(((f32[4,8,256]{2,1,0:T(8,128)}), f32[4,256,256]{2,1,0:T(8,128)}) %all-gather.4.cloned.1.call-update) | async-done | bytes 1048592 | tf_op jit(solution)/shard_map/all_gather | solution.py:88
  146.3 153.1 %all-gather.6.cloned.1.call-done = f32[4,256,256]{2,1,0:T(8,128)} async-done(((f32[4,8,256]{2,1,0:T(8,128)}), f32[4,256,256]{2,1,0:T(8,128)}) %all-gather.6.cloned.1.call-update) | async-done | bytes 1048592 | tf_op jit(solution)/shard_map/all_gather | solution.py:87
  299.4 141.4 %while.89 = (s32[]{:T(128)}, f32[256,256]{1,0:T(8,128)S(1)}, f32[4,256,256]{2,1,0:T(8,128)}, f32[4,256,256]{2,1,0:T(8,128)S(1)}, f32[4,256,256]{2,1,0:T(8,128)S(...) while((s32[]{:T(128)}, f32[256,256]{1,0:T(8,128)S(1)}, f32[4,256,256]{2,1,0:T(8,128)}, ...), condition=%wide.region_3.4_spmd, body=%wide.region_0.3_spmd.sunk | while | flops 402718720 | bytes 3409166 | solution.py:98
  306.4 27.2 %collective-permute-start.1 = (f32[256,256]{1,0:T(8,128)S(1)}, f32[256,256]{1,0:T(8,128)S(1)}, u32[]{:S(2)}, u32[]{:S(2)}) collective-permute-start(f32[256,256]{1,0:T(8,128)S(1)} %get-tuple-element.703), channel_id=1, source_target_pairs={{0,1},{1,2},{2,3},{3,4},{4,5},{5,6},{6,7},{8,9},{9,10},{10,11},{11... | collective-permute-start | bytes 786440 | tf_op jit(solution)/shard_map/while/body/eval_jaxpr/ppermute | solution.py:13
  404.9 7.0 %while.94 = (s32[]{:T(128)}, f32[256,256]{1,0:T(8,128)S(1)}, f32[4,256,256]{2,1,0:T(8,128)}, f32[4,256,256]{2,1,0:T(8,128)S(1)}, f32[4,256,256]{2,1,0:T(8,128)S(1)}, /*index=5*/s32[]{:T(128)}) while((s32[]{:T(128)}, f32[256,256]{1,0:T(8,128)S(1)}, f32[4,256,256]{2,1,0:T(8,128)}, f32[4,256,256]{2,1,0:T(8,128)S(1)}, ...), condition=%wide.region_2.2_spmd, body=%wide.region_1.1_spmd.sunk | while | flops 402718720 | bytes 1836113 | solution.py:49
  428.6 7.2 %collective-permute-start.1 = (f32[256,256]{1,0:T(8,128)S(1)}, f32[256,256]{1,0:T(8,128)S(1)}, u32[]{:S(2)}, u32[]{:S(2)}) collective-permute-start(f32[256,256]{1,0:T(8,128)S(1)} %get-tuple-element.703), channel_id=1, source_target_pairs={{0,1},{1,2},{2,3},{3,4},{4,5},{5,6},{6,7},{8,9},{9,10},{10,11},{11... | collective-permute-start | bytes 786440 | tf_op jit(solution)/shard_map/while/body/eval_jaxpr/ppermute | solution.py:13
  440.9 7.0 %while.90 = (s32[]{:T(128)}, f32[256,256]{1,0:T(8,128)S(1)}, f32[4,256,256]{2,1,0:T(8,128)S(1)}, f32[4,256,256]{2,1,0:T(8,128)}, f32[4,256,256]{2,1,0:T(8,128)S(1)}, /*index=5*/f32[4,256,256]{2,1,0:T(8,128)S(1)}, s32[]{:T(128)}) while((s32[]{:T(128)}, f32[256,256]{1,0:T(8,128)S(1)}, f32[4,256,256]{2,1,0:T(8,128)S(1)}, ...), condition=%wide.region_5.6_spmd, body=%wide.region_4.5_spmd.sunk | while | flops 402718720 | bytes 2099285 | solution.py:49
  447.9 138.3 %while.92 = (s32[]{:T(128)}, f32[256,256]{1,0:T(8,128)S(1)}, f32[4,256,256]{2,1,0:T(8,128)S(1)}, f32[4,256,256]{2,1,0:T(8,128)}, f32[4,256,256]{2,1,0:T(8,128)S(...) while((s32[]{:T(128)}, f32[256,256]{1,0:T(8,128)S(1)}, f32[4,256,256]{2,1,0:T(8,128)S(1)}, ...), condition=%wide.region_9.10_spmd, body=%wide.region_6.9_spmd.sunk | while | flops 402718720 | bytes 3409194 | solution.py:105
  447.9 8.7 %while.95 = (s32[]{:T(128)}, f32[256,256]{1,0:T(8,128)S(1)}, f32[4,256,256]{2,1,0:T(8,128)S(1)}, f32[4,256,256]{2,1,0:T(8,128)}, f32[4,256,256]{2,1,0:T(8,128)S(1)}, /*index=5*/s32[]{:T(128)}, s32[]{:T(128)}) while((s32[]{:T(128)}, f32[256,256]{1,0:T(8,128)S(1)}, f32[4,256,256]{2,1,0:T(8,128)S(1)}, f32[4,256,256]{2,1,0:T(8,128)}, ...), condition=%wide.region_8.8_spmd, body=%wide.region_7.7_spmd.sunk | while | flops 402718720 | bytes 1836133 | solution.py:63
  458.6 7.9 %collective-permute-done = f32[256,256]{1,0:T(8,128)} collective-permute-done((f32[256,256]{1,0:T(8,128)S(1)}, f32[256,256]{1,0:T(8,128)}, u32[]{:S(2)}, u32[]{:S(2)}) %collective-permute-start) | collective-permute-done | bytes 262176 | tf_op jit(solution)/shard_map/while/body/eval_jaxpr/ppermute | solution.py:13
  467.4 8.7 %while.95 = (s32[]{:T(128)}, f32[256,256]{1,0:T(8,128)S(1)}, f32[4,256,256]{2,1,0:T(8,128)S(1)}, f32[4,256,256]{2,1,0:T(8,128)}, f32[4,256,256]{2,1,0:T(8,128)S(1)}, /*index=5*/s32[]{:T(128)}, s32[]{:T(128)}) while((s32[]{:T(128)}, f32[256,256]{1,0:T(8,128)S(1)}, f32[4,256,256]{2,1,0:T(8,128)S(1)}, f32[4,256,256]{2,1,0:T(8,128)}, ...), condition=%wide.region_8.8_spmd, body=%wide.region_7.7_spmd.sunk | while | flops 402718720 | bytes 1836133 | solution.py:63
  478.1 8.3 %collective-permute-done = f32[256,256]{1,0:T(8,128)} collective-permute-done((f32[256,256]{1,0:T(8,128)S(1)}, f32[256,256]{1,0:T(8,128)}, u32[]{:S(2)}, u32[]{:S(2)}) %collective-permute-start) | collective-permute-done | bytes 262176 | tf_op jit(solution)/shard_map/while/body/eval_jaxpr/ppermute | solution.py:13
  487.3 8.7 %while.95 = (s32[]{:T(128)}, f32[256,256]{1,0:T(8,128)S(1)}, f32[4,256,256]{2,1,0:T(8,128)S(1)}, f32[4,256,256]{2,1,0:T(8,128)}, f32[4,256,256]{2,1,0:T(8,128)S(1)}, /*index=5*/s32[]{:T(128)}, s32[]{:T(128)}) while((s32[]{:T(128)}, f32[256,256]{1,0:T(8,128)S(1)}, f32[4,256,256]{2,1,0:T(8,128)S(1)}, f32[4,256,256]{2,1,0:T(8,128)}, ...), condition=%wide.region_8.8_spmd, body=%wide.region_7.7_spmd.sunk | while | flops 402718720 | bytes 1836133 | solution.py:63
  497.9 9.0 %collective-permute-done = f32[256,256]{1,0:T(8,128)} collective-permute-done((f32[256,256]{1,0:T(8,128)S(1)}, f32[256,256]{1,0:T(8,128)}, u32[]{:S(2)}, u32[]{:S(2)}) %collective-permute-start) | collective-permute-done | bytes 262176 | tf_op jit(solution)/shard_map/while/body/eval_jaxpr/ppermute | solution.py:13
  507.9 8.7 %while.95 = (s32[]{:T(128)}, f32[256,256]{1,0:T(8,128)S(1)}, f32[4,256,256]{2,1,0:T(8,128)S(1)}, f32[4,256,256]{2,1,0:T(8,128)}, f32[4,256,256]{2,1,0:T(8,128)S(1)}, /*index=5*/s32[]{:T(128)}, s32[]{:T(128)}) while((s32[]{:T(128)}, f32[256,256]{1,0:T(8,128)S(1)}, f32[4,256,256]{2,1,0:T(8,128)S(1)}, f32[4,256,256]{2,1,0:T(8,128)}, ...), condition=%wide.region_8.8_spmd, body=%wide.region_7.7_spmd.sunk | while | flops 402718720 | bytes 1836133 | solution.py:63
  518.5 8.0 %collective-permute-done = f32[256,256]{1,0:T(8,128)} collective-permute-done((f32[256,256]{1,0:T(8,128)S(1)}, f32[256,256]{1,0:T(8,128)}, u32[]{:S(2)}, u32[]{:S(2)}) %collective-permute-start) | collective-permute-done | bytes 262176 | tf_op jit(solution)/shard_map/while/body/eval_jaxpr/ppermute | solution.py:13
  527.5 8.7 %while.95 = (s32[]{:T(128)}, f32[256,256]{1,0:T(8,128)S(1)}, f32[4,256,256]{2,1,0:T(8,128)S(1)}, f32[4,256,256]{2,1,0:T(8,128)}, f32[4,256,256]{2,1,0:T(8,128)S(1)}, /*index=5*/s32[]{:T(128)}, s32[]{:T(128)}) while((s32[]{:T(128)}, f32[256,256]{1,0:T(8,128)S(1)}, f32[4,256,256]{2,1,0:T(8,128)S(1)}, f32[4,256,256]{2,1,0:T(8,128)}, ...), condition=%wide.region_8.8_spmd, body=%wide.region_7.7_spmd.sunk | while | flops 402718720 | bytes 1836133 | solution.py:63
  538.1 8.0 %collective-permute-done = f32[256,256]{1,0:T(8,128)} collective-permute-done((f32[256,256]{1,0:T(8,128)S(1)}, f32[256,256]{1,0:T(8,128)}, u32[]{:S(2)}, u32[]{:S(2)}) %collective-permute-start) | collective-permute-done | bytes 262176 | tf_op jit(solution)/shard_map/while/body/eval_jaxpr/ppermute | solution.py:13
  547.0 8.7 %while.95 = (s32[]{:T(128)}, f32[256,256]{1,0:T(8,128)S(1)}, f32[4,256,256]{2,1,0:T(8,128)S(1)}, f32[4,256,256]{2,1,0:T(8,128)}, f32[4,256,256]{2,1,0:T(8,128)S(1)}, /*index=5*/s32[]{:T(128)}, s32[]{:T(128)}) while((s32[]{:T(128)}, f32[256,256]{1,0:T(8,128)S(1)}, f32[4,256,256]{2,1,0:T(8,128)S(1)}, f32[4,256,256]{2,1,0:T(8,128)}, ...), condition=%wide.region_8.8_spmd, body=%wide.region_7.7_spmd.sunk | while | flops 402718720 | bytes 1836133 | solution.py:63
  557.7 8.0 %collective-permute-done = f32[256,256]{1,0:T(8,128)} collective-permute-done((f32[256,256]{1,0:T(8,128)S(1)}, f32[256,256]{1,0:T(8,128)}, u32[]{:S(2)}, u32[]{:S(2)}) %collective-permute-start) | collective-permute-done | bytes 262176 | tf_op jit(solution)/shard_map/while/body/eval_jaxpr/ppermute | solution.py:13
  566.6 8.7 %while.95 = (s32[]{:T(128)}, f32[256,256]{1,0:T(8,128)S(1)}, f32[4,256,256]{2,1,0:T(8,128)S(1)}, f32[4,256,256]{2,1,0:T(8,128)}, f32[4,256,256]{2,1,0:T(8,128)S(1)}, /*index=5*/s32[]{:T(128)}, s32[]{:T(128)}) while((s32[]{:T(128)}, f32[256,256]{1,0:T(8,128)S(1)}, f32[4,256,256]{2,1,0:T(8,128)S(1)}, f32[4,256,256]{2,1,0:T(8,128)}, ...), condition=%wide.region_8.8_spmd, body=%wide.region_7.7_spmd.sunk | while | flops 402718720 | bytes 1836133 | solution.py:63
  577.3 8.0 %collective-permute-done = f32[256,256]{1,0:T(8,128)} collective-permute-done((f32[256,256]{1,0:T(8,128)S(1)}, f32[256,256]{1,0:T(8,128)}, u32[]{:S(2)}, u32[]{:S(2)}) %collective-permute-start) | collective-permute-done | bytes 262176 | tf_op jit(solution)/shard_map/while/body/eval_jaxpr/ppermute | solution.py:13
  587.3 11.5 %while.93 = (s32[]{:T(128)}, f32[256,256]{1,0:T(8,128)S(1)}, f32[4,256,256]{2,1,0:T(8,128)}, f32[4,256,256]{2,1,0:T(8,128)S(1)}, f32[4,256,256]{2,1,0:T(8,128)},...) while((s32[]{:T(128)}, f32[256,256]{1,0:T(8,128)S(1)}, f32[4,256,256]{2,1,0:T(8,128)}, ...), condition=%wide.region_11.12_spmd, body=%wide.region_10.11_spmd.sunk | while | flops 402718720 | bytes 2098797 | solution.py:63
  608.9 9.5 %collective-permute-done.3 = f32[256,256]{1,0:T(8,128)S(1)} collective-permute-done((f32[256,256]{1,0:T(8,128)S(1)}, f32[256,256]{1,0:T(8,128)S(1)}, u32[]{:S(2)}, u32[]{:S(2)}) %collective-permute-start.3) | collective-permute-done | bytes 262176 | tf_op jit(solution)/shard_map/ppermute | solution.py:26
  (199 shorter events, 280.5 us)
Async XLA Ops:
  7.2 137.5 %all-gather.4.cloned.1.call-start = ((), (), s32[]{:S(2)}) async-start(), calls=%async_computation | async-start | bytes 1081344 | tf_op jit(solution)/shard_map/all_gather | solution.py:88
  7.9 291.5 %all-gather.6.cloned.1.call-start = ((), (), s32[]{:S(2)}) async-start(), calls=%async_computation.1 | async-start | bytes 1081344 | tf_op jit(solution)/shard_map/all_gather | solution.py:87
  8.6 611.3 %all-gather.8.cloned.1.call-start = ((), (), s32[]{:S(2)}) async-start(), calls=%async_computation.2 | async-start | bytes 3244032 | tf_op jit(solution)/shard_map/all_gather | solution.py:114
  11.3 288.1 %copy-start = (f32[1024,256]{1,0:T(8,128)S(1)}, f32[1024,256]{1,0:T(8,128)}, u32[]{:S(2)}) copy-start(f32[1024,256]{1,0:T(8,128)} %param.18) | copy-start | bytes 3145732
  306.4 31.6 %collective-permute-start.1 = (f32[256,256]{1,0:T(8,128)S(1)}, f32[256,256]{1,0:T(8,128)S(1)}, u32[]{:S(2)}, u32[]{:S(2)}) collective-permute-start(f32[256,256]{1,0:T(8,128)S(1)} %get-tuple-element.703), channel_id=1, source_target_pairs={{0,1},{1,2},{2,3},{3,4},{4,5},{5,6},{6,7},{8,9},{9,10},{10,11},{11... | collective-permute-start | bytes 786440 | tf_op jit(solution)/shard_map/while/body/eval_jaxpr/ppermute | solution.py:13
  345.1 9.8 %collective-permute-start.1 = (f32[256,256]{1,0:T(8,128)S(1)}, f32[256,256]{1,0:T(8,128)S(1)}, u32[]{:S(2)}, u32[]{:S(2)}) collective-permute-start(f32[256,256]{1,0:T(8,128)S(1)} %get-tuple-element.703), channel_id=1, source_target_pairs={{0,1},{1,2},{2,3},{3,4},{4,5},{5,6},{6,7},{8,9},{9,10},{10,11},{11... | collective-permute-start | bytes 786440 | tf_op jit(solution)/shard_map/while/body/eval_jaxpr/ppermute | solution.py:13
  361.8 9.2 %collective-permute-start.1 = (f32[256,256]{1,0:T(8,128)S(1)}, f32[256,256]{1,0:T(8,128)S(1)}, u32[]{:S(2)}, u32[]{:S(2)}) collective-permute-start(f32[256,256]{1,0:T(8,128)S(1)} %get-tuple-element.703), channel_id=1, source_target_pairs={{0,1},{1,2},{2,3},{3,4},{4,5},{5,6},{6,7},{8,9},{9,10},{10,11},{11... | collective-permute-start | bytes 786440 | tf_op jit(solution)/shard_map/while/body/eval_jaxpr/ppermute | solution.py:13
  378.0 10.7 %collective-permute-start.1 = (f32[256,256]{1,0:T(8,128)S(1)}, f32[256,256]{1,0:T(8,128)S(1)}, u32[]{:S(2)}, u32[]{:S(2)}) collective-permute-start(f32[256,256]{1,0:T(8,128)S(1)} %get-tuple-element.703), channel_id=1, source_target_pairs={{0,1},{1,2},{2,3},{3,4},{4,5},{5,6},{6,7},{8,9},{9,10},{10,11},{11... | collective-permute-start | bytes 786440 | tf_op jit(solution)/shard_map/while/body/eval_jaxpr/ppermute | solution.py:13
  395.8 9.1 %collective-permute-start.1 = (f32[256,256]{1,0:T(8,128)S(1)}, f32[256,256]{1,0:T(8,128)S(1)}, u32[]{:S(2)}, u32[]{:S(2)}) collective-permute-start(f32[256,256]{1,0:T(8,128)S(1)} %get-tuple-element.703), channel_id=1, source_target_pairs={{0,1},{1,2},{2,3},{3,4},{4,5},{5,6},{6,7},{8,9},{9,10},{10,11},{11... | collective-permute-start | bytes 786440 | tf_op jit(solution)/shard_map/while/body/eval_jaxpr/ppermute | solution.py:13
  411.9 9.6 %collective-permute-start.1 = (f32[256,256]{1,0:T(8,128)S(1)}, f32[256,256]{1,0:T(8,128)S(1)}, u32[]{:S(2)}, u32[]{:S(2)}) collective-permute-start(f32[256,256]{1,0:T(8,128)S(1)} %get-tuple-element.703), channel_id=1, source_target_pairs={{0,1},{1,2},{2,3},{3,4},{4,5},{5,6},{6,7},{8,9},{9,10},{10,11},{11... | collective-permute-start | bytes 786440 | tf_op jit(solution)/shard_map/while/body/eval_jaxpr/ppermute | solution.py:13
  428.6 12.2 %collective-permute-start.1 = (f32[256,256]{1,0:T(8,128)S(1)}, f32[256,256]{1,0:T(8,128)S(1)}, u32[]{:S(2)}, u32[]{:S(2)}) collective-permute-start(f32[256,256]{1,0:T(8,128)S(1)} %get-tuple-element.703), channel_id=1, source_target_pairs={{0,1},{1,2},{2,3},{3,4},{4,5},{5,6},{6,7},{8,9},{9,10},{10,11},{11... | collective-permute-start | bytes 786440 | tf_op jit(solution)/shard_map/while/body/eval_jaxpr/ppermute | solution.py:13
  456.7 9.8 %collective-permute-start = (f32[256,256]{1,0:T(8,128)S(1)}, f32[256,256]{1,0:T(8,128)}, u32[]{:S(2)}, u32[]{:S(2)}) collective-permute-start(f32[256,256]{1,0:T(8,128)S(1)} %get-tuple-element.718), channel_id=1, source_target_pairs={{1,0},{2,1},{3,2},{4,3},{5,4},{6,5},{7,6},{9,8},{10,9},{11,10},{12... | collective-permute-start | bytes 786440 | tf_op jit(solution)/shard_map/while/body/eval_jaxpr/ppermute | solution.py:13
  476.2 10.2 %collective-permute-start = (f32[256,256]{1,0:T(8,128)S(1)}, f32[256,256]{1,0:T(8,128)}, u32[]{:S(2)}, u32[]{:S(2)}) collective-permute-start(f32[256,256]{1,0:T(8,128)S(1)} %get-tuple-element.718), channel_id=1, source_target_pairs={{1,0},{2,1},{3,2},{4,3},{5,4},{6,5},{7,6},{9,8},{10,9},{11,10},{12... | collective-permute-start | bytes 786440 | tf_op jit(solution)/shard_map/while/body/eval_jaxpr/ppermute | solution.py:13
  496.0 10.9 %collective-permute-start = (f32[256,256]{1,0:T(8,128)S(1)}, f32[256,256]{1,0:T(8,128)}, u32[]{:S(2)}, u32[]{:S(2)}) collective-permute-start(f32[256,256]{1,0:T(8,128)S(1)} %get-tuple-element.718), channel_id=1, source_target_pairs={{1,0},{2,1},{3,2},{4,3},{5,4},{6,5},{7,6},{9,8},{10,9},{11,10},{12... | collective-permute-start | bytes 786440 | tf_op jit(solution)/shard_map/while/body/eval_jaxpr/ppermute | solution.py:13
  516.6 9.9 %collective-permute-start = (f32[256,256]{1,0:T(8,128)S(1)}, f32[256,256]{1,0:T(8,128)}, u32[]{:S(2)}, u32[]{:S(2)}) collective-permute-start(f32[256,256]{1,0:T(8,128)S(1)} %get-tuple-element.718), channel_id=1, source_target_pairs={{1,0},{2,1},{3,2},{4,3},{5,4},{6,5},{7,6},{9,8},{10,9},{11,10},{12... | collective-permute-start | bytes 786440 | tf_op jit(solution)/shard_map/while/body/eval_jaxpr/ppermute | solution.py:13
  536.2 9.9 %collective-permute-start = (f32[256,256]{1,0:T(8,128)S(1)}, f32[256,256]{1,0:T(8,128)}, u32[]{:S(2)}, u32[]{:S(2)}) collective-permute-start(f32[256,256]{1,0:T(8,128)S(1)} %get-tuple-element.718), channel_id=1, source_target_pairs={{1,0},{2,1},{3,2},{4,3},{5,4},{6,5},{7,6},{9,8},{10,9},{11,10},{12... | collective-permute-start | bytes 786440 | tf_op jit(solution)/shard_map/while/body/eval_jaxpr/ppermute | solution.py:13
  555.8 9.9 %collective-permute-start = (f32[256,256]{1,0:T(8,128)S(1)}, f32[256,256]{1,0:T(8,128)}, u32[]{:S(2)}, u32[]{:S(2)}) collective-permute-start(f32[256,256]{1,0:T(8,128)S(1)} %get-tuple-element.718), channel_id=1, source_target_pairs={{1,0},{2,1},{3,2},{4,3},{5,4},{6,5},{7,6},{9,8},{10,9},{11,10},{12... | collective-permute-start | bytes 786440 | tf_op jit(solution)/shard_map/while/body/eval_jaxpr/ppermute | solution.py:13
  575.3 9.9 %collective-permute-start = (f32[256,256]{1,0:T(8,128)S(1)}, f32[256,256]{1,0:T(8,128)}, u32[]{:S(2)}, u32[]{:S(2)}) collective-permute-start(f32[256,256]{1,0:T(8,128)S(1)} %get-tuple-element.718), channel_id=1, source_target_pairs={{1,0},{2,1},{3,2},{4,3},{5,4},{6,5},{7,6},{9,8},{10,9},{11,10},{12... | collective-permute-start | bytes 786440 | tf_op jit(solution)/shard_map/while/body/eval_jaxpr/ppermute | solution.py:13
  587.3 20.5 %copy-start.2 = (s32[4,4,12]{2,1,0:T(4,128)S(1)}, s32[4,4,12]{2,1,0:T(4,128)}, u32[]{:S(2)}) copy-start(s32[4,4,12]{2,1,0:T(4,128)} %param.23) | copy-start | bytes 2308
  599.9 9.1 %collective-permute-start.2 = (f32[256,256]{1,0:T(8,128)S(1)}, f32[256,256]{1,0:T(8,128)S(1)}, u32[]{:S(2)}, u32[]{:S(2)}) collective-permute-start(f32[256,256]{1,0:T(8,128)S(1)} %get-tuple-element.504), channel_id=1, source_target_pairs={{0,1},{1,2},{2,3},{3,4},{4,5},{5,6},{6,7},{8,9},{9,10},{10,11},{11... | collective-permute-start | bytes 786440 | tf_op jit(solution)/shard_map/ppermute | solution.py:24
  605.6 12.8 %collective-permute-start.3 = (f32[256,256]{1,0:T(8,128)S(1)}, f32[256,256]{1,0:T(8,128)S(1)}, u32[]{:S(2)}, u32[]{:S(2)}) collective-permute-start(f32[256,256]{1,0:T(8,128)S(1)} %get-tuple-element.505), channel_id=1, source_target_pairs={{1,0},{2,1},{3,2},{4,3},{5,4},{6,5},{7,6},{9,8},{10,9},{11,10},{12... | collective-permute-start | bytes 786440 | tf_op jit(solution)/shard_map/ppermute | solution.py:26
  624.8 2.2 copy-start.1
Sparse Core Ops, SparseCore 0:
  9.8 134.8 all-gather.3
  146.4 152.9 all-gather.5
  301.2 158.2 all-gather.7
where the time goes:
time: 643 us; the launch traced here: 640 us
  waiting for transfers between devices  384 us (60%)
  matrix products  133 us (21%)
  starting transfers between devices  82.5 us (13%)
  local copies, waits for them, and re-layouts  17.9 us (3%)
  between operations  13.9 us (2%)
    all_gather x1, waiting for transfers between devices, on_device(): lax.all_gather(diag_inv, 'rhs', axis=1, tiled=True)  153 us
    all_gather x1, waiting for transfers between devices, on_device(): lax.all_gather(lower, 'rhs', axis=1, tiled=True)  131 us
    ppermute x14, waiting for transfers between devices, shifted(): lax.ppermute(value, axis, [(source, source + steps) for source in range(i...  88.2 us
    ppermute x14, starting transfers between devices, shifted(): lax.ppermute(value, axis, [(source, source + steps) for source in range(i...  74.5 us
    dot_general x32, matrix products, advance(): lax.dot_general(inv_block, forward_block - entering, TRANSPOSED, precisio...  52.3 us
    dot_general x32, matrix products, advance(): solved = jnp.dot(inv_block, rhs_block - coupled, precision=HIGHEST_PREC)  42.7 us
    dot_general x32, matrix products, advance(): lax.dot_general(low_block, solved, TRANSPOSED, precision=HIGHEST_PREC)  19.3 us
  transfers between devices with their start and end apart: 19, of which 18 were waited for; matrix products, arithmetic and copies ran while one was open for 22% of the time, Pallas kernels for 0%

commit v1 on v0

--- a/solution.py
+++ b/solution.py
@@ -83,8 +83,12 @@
     panel_rows = diag_inv.shape[2]
     columns = right_side.shape[1]
     rhs_blocks = right_side.reshape(supers, panel_rows, columns)
+    solve_object_all = lambda vector, bus_axis, which_dim: jnp.concatenate(
+        jax.lax.all_to_all(jnp.stack(jax.lax.psum(1, bus_axis) * [vector], axis=0), bus_axis, 0, 0),
+        which_dim,
+    )
     inverse, lower_all = (
-        lax.all_gather(diag_inv, "rhs", axis=1, tiled=True),
+        solve_object_all(diag_inv, "rhs", 1),
         lax.all_gather(lower, "rhs", axis=1, tiled=True),
     )
     masked = apply_pattern(lower_all, factor_pattern)

time: 643 us -> 468 us (0.73)
  waiting for transfers between devices: 384 us -> 224 us
  matrix products: 133 us -> 106 us
  local copies, waits for them, and re-layouts: 17.9 us -> 26.5 us
    all_gather x1 -> x0, waiting for transfers between devices: 153 us -> none  [on_device(): lax.all_gather(diag_inv, 'rhs', axis=1, tiled=True)]
    dot_general x32, matrix products: 42.7 us -> 15.1 us  [advance(): solved = jnp.dot(inv_block, rhs_block - coupled, precision=HIGHEST_PREC)]
    all_gather x1, waiting for transfers between devices: 131 us -> 116 us  [on_device(): lax.all_gather(lower, 'rhs', axis=1, tiled=True)]
    all_to_all x0 -> x1, waiting for transfers between devices: none -> 12.3 us  [on_device(): jax.lax.all_to_all(jnp.stack(jax.lax.psum(1, bus_axis) * [vector], axis=0...]
    all_to_all x0 -> x1, starting transfers between devices: none -> 9.21 us  [on_device(): jax.lax.all_to_all(jnp.stack(jax.lax.psum(1, bus_axis) * [vector], axis=0...]
    while x14, local copies, waits for them, and re-layouts: 6.78 us -> 13.3 us
  transfers between devices with their start and end apart: 19 -> 19, of which waited for: 18 -> 18; matrix products, arithmetic and copies ran while one was open for 22% -> 27% of each run, Pallas kernels for 0% -> 0%
where the time goes in v1:
time: 468 us; the launch traced here: 466 us
  waiting for transfers between devices  224 us (48%)
  matrix products  106 us (23%)
  starting transfers between devices  88.7 us (19%)
  local copies, waits for them, and re-layouts  26.5 us (6%)
  between operations  14.2 us (3%)
  other arithmetic  5.41 us (1%)
    all_gather x1, waiting for transfers between devices, on_device(): lax.all_gather(lower, 'rhs', axis=1, tiled=True)  116 us
    ppermute x14, waiting for transfers between devices, shifted(): lax.ppermute(value, axis, [(source, source + steps) for source in range(i...  84.1 us
    ppermute x14, starting transfers between devices, shifted(): lax.ppermute(value, axis, [(source, source + steps) for source in range(i...  71.6 us
    dot_general x32, matrix products, advance(): lax.dot_general(inv_block, forward_block - entering, TRANSPOSED, precisio...  52.4 us
    dot_general x32, matrix products, advance(): lax.dot_general(low_block, solved, TRANSPOSED, precision=HIGHEST_PREC)  19.3 us
    dot_general x32, matrix products, advance(): solved = jnp.dot(inv_block, rhs_block - coupled, precision=HIGHEST_PREC)  15.1 us
    while x14, local copies, waits for them, and re-layouts  13.3 us
    all_to_all x1, waiting for transfers between devices, on_device(): jax.lax.all_to_all(jnp.stack(jax.lax.psum(1, bus_axis) * [vector], axis=0...  12.3 us
  transfers between devices with their start and end apart: 19, of which 18 were waited for; matrix products, arithmetic and copies ran while one was open for 27% of the time, Pallas kernels for 0%

profile of v1, /device:TPU:1, one launch (start us, length us, event | category | flops | bytes accessed | tf_op | source)
XLA Modules:
  0.0 466.0 jit_solution(3806899379153327105)
XLA Ops:
  9.8 9.2 %all-to-all-start = ((f32[32,4,8,256]{3,2,1,0:T(8,128)}), f32[32,4,8,256]{3,2,1,0:T(8,128)S(1)}, u32[]{:S(2)}, u32[]{:S(2)}) async-start(f32[32,4,8,256]{3,2,1,0:T(8,128)} %stack.2), calls=%async_computation | async-start | bytes 2097152 | tf_op jit(solution)/shard_map/all_to_all | solution.py:87
  22.2 12.3 %all-to-all-done = f32[32,4,8,256]{3,2,1,0:T(8,128)S(1)} async-done(((f32[32,4,8,256]{3,2,1,0:T(8,128)}), f32[32,4,8,256]{3,2,1,0:T(8,128)S(1)}, u32[]{:S(2)}, u32[]{:S(2)}) %all-to-all-start) | async-done | bytes 1048608 | tf_op jit(solution)/shard_map/all_to_all | solution.py:87
  34.6 116.2 %all-gather.3.cloned.1.call-done = f32[4,256,256]{2,1,0:T(8,128)} async-done(((f32[4,8,256]{2,1,0:T(8,128)}), f32[4,256,256]{2,1,0:T(8,128)}) %all-gather.3.cloned.1.call-update) | async-done | bytes 1048592 | tf_op jit(solution)/shard_map/all_gather | solution.py:92
  152.5 116.7 %while.89 = (s32[]{:T(128)}, f32[256,256]{1,0:T(8,128)S(1)}, f32[4,256,256]{2,1,0:T(8,128)S(1)}, f32[4,256,256]{2,1,0:T(8,128)S(1)}, f32[4,256,256]{2,1,0:T(8,12...) while((s32[]{:T(128)}, f32[256,256]{1,0:T(8,128)S(1)}, f32[4,256,256]{2,1,0:T(8,128)S(1)}, ...), condition=%wide.region_3.4_spmd, body=%wide.region_0.3_spmd.sunk | while | flops 402718720 | bytes 3409166 | solution.py:102
  155.7 25.6 %collective-permute-start.1 = (f32[256,256]{1,0:T(8,128)S(1)}, f32[256,256]{1,0:T(8,128)}, u32[]{:S(2)}, u32[]{:S(2)}) collective-permute-start(f32[256,256]{1,0:T(8,128)S(1)} %get-tuple-element.703), channel_id=1, source_target_pairs={{0,1},{1,2},{2,3},{3,4},{4,5},{5,6},{6,7},{8,9},{9,10},{10,11},{11... | collective-permute-start | bytes 786440 | tf_op jit(solution)/shard_map/while/body/eval_jaxpr/ppermute | solution.py:13
  270.3 5.9 %while.90 = (s32[]{:T(128)}, f32[256,256]{1,0:T(8,128)S(1)}, f32[4,256,256]{2,1,0:T(8,128)}, f32[4,256,256]{2,1,0:T(8,128)S(1)}, f32[4,256,256]{2,1,0:T(8,128)S(1)}, /*index=5*/f32[4,256,256]{2,1,0:T(8,128)S(1)}, s32[]{:T(128)}) while((s32[]{:T(128)}, f32[256,256]{1,0:T(8,128)S(1)}, f32[4,256,256]{2,1,0:T(8,128)}, ...), condition=%wide.region_5.6_spmd, body=%wide.region_4.5_spmd.sunk | while | flops 402718720 | bytes 2099285 | solution.py:49
  276.2 135.7 %while.92 = (s32[]{:T(128)}, f32[256,256]{1,0:T(8,128)S(1)}, f32[4,256,256]{2,1,0:T(8,128)S(1)}, f32[4,256,256]{2,1,0:T(8,128)S(1)}, f32[4,256,256]{2,1,0:T(8,12...) while((s32[]{:T(128)}, f32[256,256]{1,0:T(8,128)S(1)}, f32[4,256,256]{2,1,0:T(8,128)S(1)}, ...), condition=%wide.region_9.10_spmd, body=%wide.region_6.9_spmd.sunk | while | flops 402718720 | bytes 3409194 | solution.py:109
  276.2 8.7 %while.95 = (s32[]{:T(128)}, f32[256,256]{1,0:T(8,128)S(1)}, f32[4,256,256]{2,1,0:T(8,128)S(1)}, f32[4,256,256]{2,1,0:T(8,128)S(1)}, f32[4,256,256]{2,1,0:T(8,128)}, /*index=5*/s32[]{:T(128)}, s32[]{:T(128)}) while((s32[]{:T(128)}, f32[256,256]{1,0:T(8,128)S(1)}, f32[4,256,256]{2,1,0:T(8,128)S(1)}, f32[4,256,256]{2,1,0:T(8,128)S(1)}, ...), condition=%wide.region_8.8_spmd, body=%wide.region_7.7_spmd.sunk | while | flops 402718720 | bytes 1836133 | solution.py:63
  286.9 8.0 %collective-permute-done = f32[256,256]{1,0:T(8,128)} collective-permute-done((f32[256,256]{1,0:T(8,128)S(1)}, f32[256,256]{1,0:T(8,128)}, u32[]{:S(2)}, u32[]{:S(2)}) %collective-permute-start) | collective-permute-done | bytes 262176 | tf_op jit(solution)/shard_map/while/body/eval_jaxpr/ppermute | solution.py:13
  295.8 8.7 %while.95 = (s32[]{:T(128)}, f32[256,256]{1,0:T(8,128)S(1)}, f32[4,256,256]{2,1,0:T(8,128)S(1)}, f32[4,256,256]{2,1,0:T(8,128)S(1)}, f32[4,256,256]{2,1,0:T(8,128)}, /*index=5*/s32[]{:T(128)}, s32[]{:T(128)}) while((s32[]{:T(128)}, f32[256,256]{1,0:T(8,128)S(1)}, f32[4,256,256]{2,1,0:T(8,128)S(1)}, f32[4,256,256]{2,1,0:T(8,128)S(1)}, ...), condition=%wide.region_8.8_spmd, body=%wide.region_7.7_spmd.sunk | while | flops 402718720 | bytes 1836133 | solution.py:63
  306.5 7.1 %collective-permute-done = f32[256,256]{1,0:T(8,128)} collective-permute-done((f32[256,256]{1,0:T(8,128)S(1)}, f32[256,256]{1,0:T(8,128)}, u32[]{:S(2)}, u32[]{:S(2)}) %collective-permute-start) | collective-permute-done | bytes 262176 | tf_op jit(solution)/shard_map/while/body/eval_jaxpr/ppermute | solution.py:13
  314.5 8.7 %while.95 = (s32[]{:T(128)}, f32[256,256]{1,0:T(8,128)S(1)}, f32[4,256,256]{2,1,0:T(8,128)S(1)}, f32[4,256,256]{2,1,0:T(8,128)S(1)}, f32[4,256,256]{2,1,0:T(8,128)}, /*index=5*/s32[]{:T(128)}, s32[]{:T(128)}) while((s32[]{:T(128)}, f32[256,256]{1,0:T(8,128)S(1)}, f32[4,256,256]{2,1,0:T(8,128)S(1)}, f32[4,256,256]{2,1,0:T(8,128)S(1)}, ...), condition=%wide.region_8.8_spmd, body=%wide.region_7.7_spmd.sunk | while | flops 402718720 | bytes 1836133 | solution.py:63
  325.2 6.8 %collective-permute-done = f32[256,256]{1,0:T(8,128)} collective-permute-done((f32[256,256]{1,0:T(8,128)S(1)}, f32[256,256]{1,0:T(8,128)}, u32[]{:S(2)}, u32[]{:S(2)}) %collective-permute-start) | collective-permute-done | bytes 262176 | tf_op jit(solution)/shard_map/while/body/eval_jaxpr/ppermute | solution.py:13
  332.9 8.7 %while.95 = (s32[]{:T(128)}, f32[256,256]{1,0:T(8,128)S(1)}, f32[4,256,256]{2,1,0:T(8,128)S(1)}, f32[4,256,256]{2,1,0:T(8,128)S(1)}, f32[4,256,256]{2,1,0:T(8,128)}, /*index=5*/s32[]{:T(128)}, s32[]{:T(128)}) while((s32[]{:T(128)}, f32[256,256]{1,0:T(8,128)S(1)}, f32[4,256,256]{2,1,0:T(8,128)S(1)}, f32[4,256,256]{2,1,0:T(8,128)S(1)}, ...), condition=%wide.region_8.8_spmd, body=%wide.region_7.7_spmd.sunk | while | flops 402718720 | bytes 1836133 | solution.py:63
  343.6 8.3 %collective-permute-done = f32[256,256]{1,0:T(8,128)} collective-permute-done((f32[256,256]{1,0:T(8,128)S(1)}, f32[256,256]{1,0:T(8,128)}, u32[]{:S(2)}, u32[]{:S(2)}) %collective-permute-start) | collective-permute-done | bytes 262176 | tf_op jit(solution)/shard_map/while/body/eval_jaxpr/ppermute | solution.py:13
  352.8 8.7 %while.95 = (s32[]{:T(128)}, f32[256,256]{1,0:T(8,128)S(1)}, f32[4,256,256]{2,1,0:T(8,128)S(1)}, f32[4,256,256]{2,1,0:T(8,128)S(1)}, f32[4,256,256]{2,1,0:T(8,128)}, /*index=5*/s32[]{:T(128)}, s32[]{:T(128)}) while((s32[]{:T(128)}, f32[256,256]{1,0:T(8,128)S(1)}, f32[4,256,256]{2,1,0:T(8,128)S(1)}, f32[4,256,256]{2,1,0:T(8,128)S(1)}, ...), condition=%wide.region_8.8_spmd, body=%wide.region_7.7_spmd.sunk | while | flops 402718720 | bytes 1836133 | solution.py:63
  363.4 8.3 %collective-permute-done = f32[256,256]{1,0:T(8,128)} collective-permute-done((f32[256,256]{1,0:T(8,128)S(1)}, f32[256,256]{1,0:T(8,128)}, u32[]{:S(2)}, u32[]{:S(2)}) %collective-permute-start) | collective-permute-done | bytes 262176 | tf_op jit(solution)/shard_map/while/body/eval_jaxpr/ppermute | solution.py:13
  372.7 8.7 %while.95 = (s32[]{:T(128)}, f32[256,256]{1,0:T(8,128)S(1)}, f32[4,256,256]{2,1,0:T(8,128)S(1)}, f32[4,256,256]{2,1,0:T(8,128)S(1)}, f32[4,256,256]{2,1,0:T(8,128)}, /*index=5*/s32[]{:T(128)}, s32[]{:T(128)}) while((s32[]{:T(128)}, f32[256,256]{1,0:T(8,128)S(1)}, f32[4,256,256]{2,1,0:T(8,128)S(1)}, f32[4,256,256]{2,1,0:T(8,128)S(1)}, ...), condition=%wide.region_8.8_spmd, body=%wide.region_7.7_spmd.sunk | while | flops 402718720 | bytes 1836133 | solution.py:63
  383.3 8.1 %collective-permute-done = f32[256,256]{1,0:T(8,128)} collective-permute-done((f32[256,256]{1,0:T(8,128)S(1)}, f32[256,256]{1,0:T(8,128)}, u32[]{:S(2)}, u32[]{:S(2)}) %collective-permute-start) | collective-permute-done | bytes 262176 | tf_op jit(solution)/shard_map/while/body/eval_jaxpr/ppermute | solution.py:13
  392.4 8.7 %while.95 = (s32[]{:T(128)}, f32[256,256]{1,0:T(8,128)S(1)}, f32[4,256,256]{2,1,0:T(8,128)S(1)}, f32[4,256,256]{2,1,0:T(8,128)S(1)}, f32[4,256,256]{2,1,0:T(8,128)}, /*index=5*/s32[]{:T(128)}, s32[]{:T(128)}) while((s32[]{:T(128)}, f32[256,256]{1,0:T(8,128)S(1)}, f32[4,256,256]{2,1,0:T(8,128)S(1)}, f32[4,256,256]{2,1,0:T(8,128)S(1)}, ...), condition=%wide.region_8.8_spmd, body=%wide.region_7.7_spmd.sunk | while | flops 402718720 | bytes 1836133 | solution.py:63
  403.0 8.0 %collective-permute-done = f32[256,256]{1,0:T(8,128)} collective-permute-done((f32[256,256]{1,0:T(8,128)S(1)}, f32[256,256]{1,0:T(8,128)}, u32[]{:S(2)}, u32[]{:S(2)}) %collective-permute-start) | collective-permute-done | bytes 262176 | tf_op jit(solution)/shard_map/while/body/eval_jaxpr/ppermute | solution.py:13
  413.0 11.5 %while.93 = (s32[]{:T(128)}, f32[256,256]{1,0:T(8,128)S(1)}, f32[4,256,256]{2,1,0:T(8,128)}, f32[4,256,256]{2,1,0:T(8,128)S(1)}, f32[4,256,256]{2,1,0:T(8,128)S(...) while((s32[]{:T(128)}, f32[256,256]{1,0:T(8,128)S(1)}, f32[4,256,256]{2,1,0:T(8,128)}, ...), condition=%wide.region_11.12_spmd, body=%wide.region_10.11_spmd.sunk | while | flops 402718720 | bytes 2098797 | solution.py:63
  434.7 9.5 %collective-permute-done.3 = f32[256,256]{1,0:T(8,128)S(1)} collective-permute-done((f32[256,256]{1,0:T(8,128)S(1)}, f32[256,256]{1,0:T(8,128)S(1)}, u32[]{:S(2)}, u32[]{:S(2)}) %collective-permute-start.3) | collective-permute-done | bytes 262176 | tf_op jit(solution)/shard_map/ppermute | solution.py:26
  452.8 6.4 %fusion.38 = f32[4,256,256]{2,1,0:T(8,128)} fusion(f32[4,256,256]{2,1,0:T(8,128)S(1)} %get-tuple-element.897, f32[4,256,768]{1,2,0:T(8,128)S(1)} %bitcast_multiply_fusion, f32[4,256,256]{2,1,0:T(8,128)S(1)} %bitcast.117, f32[4,256,256]{2,1,0:T(8,128)S(1)} %copy-done.1, f32[4,256,256]{2,1,0:T(8,128)S(1)} %bitcast.116), kind=kOutput, calls=%fused_computation.45 | convolution fusion | flops 2417754112 | bytes 8388608 | tf_op jit(solution)/shard_map/sij,sjr->sir/dot_general | solution.py:78
  (204 shorter events, 238.4 us)
Async XLA Ops:
  7.2 11.9 %copy-start.2 = (f32[4,8,768]{2,1,0:T(8,128)S(1)}, f32[4,8,768]{2,1,0:T(8,128)}, u32[]{:S(2)}) copy-start(f32[4,8,768]{2,1,0:T(8,128)} %param.22) | copy-start | bytes 294916
  7.2 12.6 %copy-start.4 = (s32[4,4,4]{2,1,0:T(4,128)S(1)}, s32[4,4,4]{2,1,0:T(4,128)}, u32[]{:S(2)}) copy-start(s32[4,4,4]{2,1,0:T(4,128)} %param.21) | copy-start | bytes 772
  7.2 143.6 %all-gather.3.cloned.1.call-start = ((), (), s32[]{:S(2)}) async-start(), calls=%async_computation.1 | async-start | bytes 1081344 | tf_op jit(solution)/shard_map/all_gather | solution.py:92
  9.8 24.7 %all-to-all-start = ((f32[32,4,8,256]{3,2,1,0:T(8,128)}), f32[32,4,8,256]{3,2,1,0:T(8,128)S(1)}, u32[]{:S(2)}, u32[]{:S(2)}) async-start(f32[32,4,8,256]{3,2,1,0:T(8,128)} %stack.2), calls=%async_computation | async-start | bytes 2097152 | tf_op jit(solution)/shard_map/all_to_all | solution.py:87
  19.0 426.7 %all-gather.5.cloned.1.call-start = ((), (), s32[]{:S(2)}) async-start(), calls=%async_computation.2 | async-start | bytes 3244032 | tf_op jit(solution)/shard_map/all_gather | solution.py:118
  22.2 130.3 %copy-start = (f32[1024,256]{1,0:T(8,128)S(1)}, f32[1024,256]{1,0:T(8,128)}, u32[]{:S(2)}) copy-start(f32[1024,256]{1,0:T(8,128)} %param.18) | copy-start | bytes 3145732
  155.7 30.0 %collective-permute-start.1 = (f32[256,256]{1,0:T(8,128)S(1)}, f32[256,256]{1,0:T(8,128)}, u32[]{:S(2)}, u32[]{:S(2)}) collective-permute-start(f32[256,256]{1,0:T(8,128)S(1)} %get-tuple-element.703), channel_id=1, source_target_pairs={{0,1},{1,2},{2,3},{3,4},{4,5},{5,6},{6,7},{8,9},{9,10},{10,11},{11... | collective-permute-start | bytes 786440 | tf_op jit(solution)/shard_map/while/body/eval_jaxpr/ppermute | solution.py:13
  189.8 9.3 %collective-permute-start.1 = (f32[256,256]{1,0:T(8,128)S(1)}, f32[256,256]{1,0:T(8,128)}, u32[]{:S(2)}, u32[]{:S(2)}) collective-permute-start(f32[256,256]{1,0:T(8,128)S(1)} %get-tuple-element.703), channel_id=1, source_target_pairs={{0,1},{1,2},{2,3},{3,4},{4,5},{5,6},{6,7},{8,9},{9,10},{10,11},{11... | collective-permute-start | bytes 786440 | tf_op jit(solution)/shard_map/while/body/eval_jaxpr/ppermute | solution.py:13
  203.3 9.9 %collective-permute-start.1 = (f32[256,256]{1,0:T(8,128)S(1)}, f32[256,256]{1,0:T(8,128)}, u32[]{:S(2)}, u32[]{:S(2)}) collective-permute-start(f32[256,256]{1,0:T(8,128)S(1)} %get-tuple-element.703), channel_id=1, source_target_pairs={{0,1},{1,2},{2,3},{3,4},{4,5},{5,6},{6,7},{8,9},{9,10},{10,11},{11... | collective-permute-start | bytes 786440 | tf_op jit(solution)/shard_map/while/body/eval_jaxpr/ppermute | solution.py:13
  217.2 10.1 %collective-permute-start.1 = (f32[256,256]{1,0:T(8,128)S(1)}, f32[256,256]{1,0:T(8,128)}, u32[]{:S(2)}, u32[]{:S(2)}) collective-permute-start(f32[256,256]{1,0:T(8,128)S(1)} %get-tuple-element.703), channel_id=1, source_target_pairs={{0,1},{1,2},{2,3},{3,4},{4,5},{5,6},{6,7},{8,9},{9,10},{10,11},{11... | collective-permute-start | bytes 786440 | tf_op jit(solution)/shard_map/while/body/eval_jaxpr/ppermute | solution.py:13
  231.5 9.0 %collective-permute-start.1 = (f32[256,256]{1,0:T(8,128)S(1)}, f32[256,256]{1,0:T(8,128)}, u32[]{:S(2)}, u32[]{:S(2)}) collective-permute-start(f32[256,256]{1,0:T(8,128)S(1)} %get-tuple-element.703), channel_id=1, source_target_pairs={{0,1},{1,2},{2,3},{3,4},{4,5},{5,6},{6,7},{8,9},{9,10},{10,11},{11... | collective-permute-start | bytes 786440 | tf_op jit(solution)/shard_map/while/body/eval_jaxpr/ppermute | solution.py:13
  244.6 10.0 %collective-permute-start.1 = (f32[256,256]{1,0:T(8,128)S(1)}, f32[256,256]{1,0:T(8,128)}, u32[]{:S(2)}, u32[]{:S(2)}) collective-permute-start(f32[256,256]{1,0:T(8,128)S(1)} %get-tuple-element.703), channel_id=1, source_target_pairs={{0,1},{1,2},{2,3},{3,4},{4,5},{5,6},{6,7},{8,9},{9,10},{10,11},{11... | collective-permute-start | bytes 786440 | tf_op jit(solution)/shard_map/while/body/eval_jaxpr/ppermute | solution.py:13
  258.6 9.6 %collective-permute-start.1 = (f32[256,256]{1,0:T(8,128)S(1)}, f32[256,256]{1,0:T(8,128)}, u32[]{:S(2)}, u32[]{:S(2)}) collective-permute-start(f32[256,256]{1,0:T(8,128)S(1)} %get-tuple-element.703), channel_id=1, source_target_pairs={{0,1},{1,2},{2,3},{3,4},{4,5},{5,6},{6,7},{8,9},{9,10},{10,11},{11... | collective-permute-start | bytes 786440 | tf_op jit(solution)/shard_map/while/body/eval_jaxpr/ppermute | solution.py:13
  285.0 9.9 %collective-permute-start = (f32[256,256]{1,0:T(8,128)S(1)}, f32[256,256]{1,0:T(8,128)}, u32[]{:S(2)}, u32[]{:S(2)}) collective-permute-start(f32[256,256]{1,0:T(8,128)S(1)} %get-tuple-element.718), channel_id=1, source_target_pairs={{1,0},{2,1},{3,2},{4,3},{5,4},{6,5},{7,6},{9,8},{10,9},{11,10},{12... | collective-permute-start | bytes 786440 | tf_op jit(solution)/shard_map/while/body/eval_jaxpr/ppermute | solution.py:13
  304.5 9.0 %collective-permute-start = (f32[256,256]{1,0:T(8,128)S(1)}, f32[256,256]{1,0:T(8,128)}, u32[]{:S(2)}, u32[]{:S(2)}) collective-permute-start(f32[256,256]{1,0:T(8,128)S(1)} %get-tuple-element.718), channel_id=1, source_target_pairs={{1,0},{2,1},{3,2},{4,3},{5,4},{6,5},{7,6},{9,8},{10,9},{11,10},{12... | collective-permute-start | bytes 786440 | tf_op jit(solution)/shard_map/while/body/eval_jaxpr/ppermute | solution.py:13
  323.3 8.7 %collective-permute-start = (f32[256,256]{1,0:T(8,128)S(1)}, f32[256,256]{1,0:T(8,128)}, u32[]{:S(2)}, u32[]{:S(2)}) collective-permute-start(f32[256,256]{1,0:T(8,128)S(1)} %get-tuple-element.718), channel_id=1, source_target_pairs={{1,0},{2,1},{3,2},{4,3},{5,4},{6,5},{7,6},{9,8},{10,9},{11,10},{12... | collective-permute-start | bytes 786440 | tf_op jit(solution)/shard_map/while/body/eval_jaxpr/ppermute | solution.py:13
  341.6 10.2 %collective-permute-start = (f32[256,256]{1,0:T(8,128)S(1)}, f32[256,256]{1,0:T(8,128)}, u32[]{:S(2)}, u32[]{:S(2)}) collective-permute-start(f32[256,256]{1,0:T(8,128)S(1)} %get-tuple-element.718), channel_id=1, source_target_pairs={{1,0},{2,1},{3,2},{4,3},{5,4},{6,5},{7,6},{9,8},{10,9},{11,10},{12... | collective-permute-start | bytes 786440 | tf_op jit(solution)/shard_map/while/body/eval_jaxpr/ppermute | solution.py:13
  361.5 10.2 %collective-permute-start = (f32[256,256]{1,0:T(8,128)S(1)}, f32[256,256]{1,0:T(8,128)}, u32[]{:S(2)}, u32[]{:S(2)}) collective-permute-start(f32[256,256]{1,0:T(8,128)S(1)} %get-tuple-element.718), channel_id=1, source_target_pairs={{1,0},{2,1},{3,2},{4,3},{5,4},{6,5},{7,6},{9,8},{10,9},{11,10},{12... | collective-permute-start | bytes 786440 | tf_op jit(solution)/shard_map/while/body/eval_jaxpr/ppermute | solution.py:13
  381.4 10.0 %collective-permute-start = (f32[256,256]{1,0:T(8,128)S(1)}, f32[256,256]{1,0:T(8,128)}, u32[]{:S(2)}, u32[]{:S(2)}) collective-permute-start(f32[256,256]{1,0:T(8,128)S(1)} %get-tuple-element.718), channel_id=1, source_target_pairs={{1,0},{2,1},{3,2},{4,3},{5,4},{6,5},{7,6},{9,8},{10,9},{11,10},{12... | collective-permute-start | bytes 786440 | tf_op jit(solution)/shard_map/while/body/eval_jaxpr/ppermute | solution.py:13
  401.1 9.9 %collective-permute-start = (f32[256,256]{1,0:T(8,128)S(1)}, f32[256,256]{1,0:T(8,128)}, u32[]{:S(2)}, u32[]{:S(2)}) collective-permute-start(f32[256,256]{1,0:T(8,128)S(1)} %get-tuple-element.718), channel_id=1, source_target_pairs={{1,0},{2,1},{3,2},{4,3},{5,4},{6,5},{7,6},{9,8},{10,9},{11,10},{12... | collective-permute-start | bytes 786440 | tf_op jit(solution)/shard_map/while/body/eval_jaxpr/ppermute | solution.py:13
  413.0 20.5 %copy-start.3 = (s32[4,4,12]{2,1,0:T(4,128)S(1)}, s32[4,4,12]{2,1,0:T(4,128)}, u32[]{:S(2)}) copy-start(s32[4,4,12]{2,1,0:T(4,128)} %param.23) | copy-start | bytes 2308
  425.6 9.0 %collective-permute-start.2 = (f32[256,256]{1,0:T(8,128)S(1)}, f32[256,256]{1,0:T(8,128)S(1)}, u32[]{:S(2)}, u32[]{:S(2)}) collective-permute-start(f32[256,256]{1,0:T(8,128)S(1)} %get-tuple-element.504), channel_id=1, source_target_pairs={{0,1},{1,2},{2,3},{3,4},{4,5},{5,6},{6,7},{8,9},{9,10},{10,11},{11... | collective-permute-start | bytes 786440 | tf_op jit(solution)/shard_map/ppermute | solution.py:24
  431.4 12.8 %collective-permute-start.3 = (f32[256,256]{1,0:T(8,128)S(1)}, f32[256,256]{1,0:T(8,128)S(1)}, u32[]{:S(2)}, u32[]{:S(2)}) collective-permute-start(f32[256,256]{1,0:T(8,128)S(1)} %get-tuple-element.505), channel_id=1, source_target_pairs={{1,0},{2,1},{3,2},{4,3},{5,4},{6,5},{7,6},{9,8},{10,9},{11,10},{12... | collective-permute-start | bytes 786440 | tf_op jit(solution)/shard_map/ppermute | solution.py:26
  450.6 2.2 copy-start.1
Sparse Core Ops, SparseCore 0:
  9.8 140.9 all-gather.2
  152.6 156.0 all-gather.4
